TPU v7x, 32 devices: a whole 2x2x4 slice. The times are simulated.
32 devices in a mesh: shard: 4 (over y, x), replica: 8 (over z, core).
Axes of the slice: x: 2, y: 2, z: 4, core: 2. Of those that a mesh axis runs over, the one named last changes fastest.
Arguments:
- hidden_in: bfloat16 [32, 212, 960], P(('shard', 'replica')), may hold values from -9 to 9
- cotangent: bfloat16 [32, 212, 960], P(('shard', 'replica')), may hold values from -6 to 6
- segment_ids: int32 [32, 212], P(('shard', 'replica')), may hold values from 0 to 6, as said below
- positions: int32 [32, 212], P(('shard', 'replica')), may hold values from 0 to 211, as said below
- w_qkv: bfloat16 [960, 1600], P(None, 'shard'), may hold values from -1 to 1
- w_out: bfloat16 [960, 960], P(None, 'shard'), may hold values from -0.5 to 0.5
- w_gate: bfloat16 [960, 2560], P(None, 'shard'), may hold values from -0.1875 to 0.1875
- w_up: bfloat16 [960, 2560], P(None, 'shard'), may hold values from -0.1875 to 0.1875
- w_down: bfloat16 [2560, 960], P('shard'), may hold values from -0.25 to 0.25
- gain_attn: bfloat16 [960], P('shard'), may hold values from 0.5 to 1.5
- gain_mlp: bfloat16 [960], P('shard'), may hold values from 0.5 to 1.5
Outputs:
- hidden_out: bfloat16 [32, 212, 960], P(('shard', 'replica'))
- grad_input: float32 [32, 212, 960], P(('shard', 'replica'))
- grad_qkv: float32 [960, 1600], P(None, 'shard')
- grad_out: float32 [960, 960], P(None, 'shard')
- grad_gate: float32 [960, 2560], P(None, 'shard')
- grad_up: float32 [960, 2560], P(None, 'shard')
- grad_down: float32 [2560, 960], P('shard')
- grad_gain_attn: float32 [960], P('shard')
- grad_gain_mlp: float32 [960], P('shard')
Inputs may be any that keep to these rules, and one draw needn't show every extreme that they name: `segment_ids`: within each sequence the numbers start at 0 and never fall; a run of equal numbers is one document. `positions`: the offset of each token from the first token of its document.
All inputs are finite; a program needn't handle non-finite values.
Results may differ from a plain program's by a relative error of at most 0.022.
Values may be sent and summed in bfloat16 or wider, within the bound.
A program may use at most 128 MiB of HBM per device.

v0:
```python
import math
import jax
import jax.numpy as jnp
from jax import lax
from jax.sharding import PartitionSpec as P

D = 960
H = 15
KV = 5
HD = 64
LEN = 212
EPSILON = 1e-05
THETA_BASE = 100000.0
NEG_FILL = -1e30


def rope_tables(position_ids):
    half_width = HD // 2
    freq_steps = jnp.arange(half_width, dtype=jnp.float32) * (2.0 / HD)
    inverse = jnp.exp(-math.log(THETA_BASE) * freq_steps)
    angles = position_ids.astype(jnp.float32)[:, None] * inverse[None, :]
    cosine = jnp.cos(angles)
    sine_part = jnp.sin(angles)
    return (jnp.concatenate([cosine, cosine], -1), jnp.concatenate([sine_part, sine_part], -1))


def rotate(tensor, cosine, sine_part):
    half_width = HD // 2
    turned = jnp.concatenate([-tensor[..., half_width:], tensor[..., :half_width]], -1)
    return tensor * cosine[:, None, :] + turned * sine_part[:, None, :]


def rotate_back(gradient, cosine, sine_part):
    half_width = HD // 2
    scaled = gradient * sine_part[:, None, :]
    return gradient * cosine[:, None, :] + jnp.concatenate(
        [scaled[..., half_width:], -scaled[..., :half_width]], -1
    )


def norm_forward(values, gain_row):
    inv_rms = lax.rsqrt(jnp.mean(values * values, -1, keepdims=True) + EPSILON)
    return ((values * inv_rms * gain_row.astype(jnp.float32)).astype(jnp.bfloat16), inv_rms)


def norm_backward(values, inv_rms, gain_row, grad_normed):
    weighted = grad_normed * gain_row.astype(jnp.float32)
    gain_grad = jnp.sum(grad_normed * values * inv_rms, 0)
    inner_mean = jnp.mean(weighted * values, -1, keepdims=True)
    return (inv_rms * weighted - values * inv_rms**3 * inner_mean, gain_grad)


def silu_parts(gate_pre):
    sigmoid_val = jax.nn.sigmoid(gate_pre)
    return (gate_pre * sigmoid_val, sigmoid_val * (1.0 + gate_pre * (1.0 - sigmoid_val)))


def attention_forward(queries, keys_in, values_in, allowed):
    length = queries.shape[0]
    groups = H // KV
    scale_factor = HD ** (-0.5)
    query_g = queries.reshape(length, KV, groups, HD)
    scores = (
        jnp.einsum("qkgd,skd->kgqs", query_g, keys_in, preferred_element_type=jnp.float32)
        * scale_factor
    )
    scores = jnp.where(allowed, scores, NEG_FILL)
    highest = jnp.max(scores, -1, keepdims=True)
    raw_weights = jnp.exp(scores - highest)
    totals = jnp.sum(raw_weights, -1, keepdims=True)
    log_total = highest + jnp.log(totals)
    attn_probs = (raw_weights / totals).astype(jnp.bfloat16)
    mixed_vals = jnp.einsum(
        "kgqs,skd->qkgd", attn_probs, values_in, preferred_element_type=jnp.float32
    )
    return (mixed_vals.reshape(length, H * HD).astype(jnp.bfloat16), log_total)


def attention_backward(queries, keys_in, values_in, allowed, log_total, attended, grad_attended):
    length = queries.shape[0]
    groups = H // KV
    scale_factor = HD ** (-0.5)
    query_g = queries.reshape(length, KV, groups, HD)
    scores = (
        jnp.einsum("qkgd,skd->kgqs", query_g, keys_in, preferred_element_type=jnp.float32)
        * scale_factor
    )
    scores = jnp.where(allowed, scores, NEG_FILL)
    attn_probs = jnp.exp(scores - log_total)
    probs_b = attn_probs.astype(jnp.bfloat16)
    grad_g = grad_attended.reshape(length, KV, groups, HD)
    attended_g = attended.reshape(length, KV, groups, HD)
    grad_values = jnp.einsum("kgqs,qkgd->skd", probs_b, grad_g, preferred_element_type=jnp.float32)
    grad_probs = jnp.einsum("qkgd,skd->kgqs", grad_g, values_in, preferred_element_type=jnp.float32)
    delta_row = jnp.sum(grad_g.astype(jnp.float32) * attended_g.astype(jnp.float32), -1)
    delta_row = jnp.transpose(delta_row, (1, 2, 0))[..., None]
    grad_scores = (attn_probs * (grad_probs - delta_row) * scale_factor).astype(jnp.bfloat16)
    grad_queries = jnp.einsum(
        "kgqs,skd->qkgd", grad_scores, keys_in, preferred_element_type=jnp.float32
    ).reshape(length, H, HD)
    grad_keys = jnp.einsum(
        "kgqs,qkgd->skd", grad_scores, query_g, preferred_element_type=jnp.float32
    )
    return (grad_queries, grad_keys, grad_values)


def on_device(
    hidden_in,
    cotangent,
    segment_ids,
    positions,
    w_qkv,
    w_out,
    w_gate,
    w_up,
    w_down,
    gain_attn,
    gain_mlp,
):
    row_total = hidden_in.shape[0] * LEN
    in_rows = hidden_in.reshape(row_total, D)
    flat_rows = in_rows.astype(jnp.float32)
    segment_row = segment_ids.reshape(row_total)
    row_index = jnp.arange(row_total)
    sequence_of = row_index // LEN
    allowed = (
        (sequence_of[:, None] == sequence_of[None, :])
        & (segment_row[:, None] == segment_row[None, :])
        & (row_index[None, :] <= row_index[:, None])
    )
    cosine, sine_part = rope_tables(positions.reshape(row_total))
    full_qkv, full_out, gain_a, gain_m = (
        lax.all_gather(w_qkv, "shard", axis=1, tiled=True),
        lax.all_gather(w_out, "shard", axis=1, tiled=True),
        lax.all_gather(gain_attn, "shard", axis=0, tiled=True),
        lax.all_gather(gain_mlp, "shard", axis=0, tiled=True),
    )
    normed_one, inv_one = norm_forward(flat_rows, gain_a)
    projected = jnp.dot(normed_one, full_qkv, preferred_element_type=jnp.float32)
    queries = rotate(projected[:, : H * HD].reshape(row_total, H, HD), cosine, sine_part).astype(
        jnp.bfloat16
    )
    keys_b = rotate(
        projected[:, H * HD : (H + KV) * HD].reshape(row_total, KV, HD), cosine, sine_part
    ).astype(jnp.bfloat16)
    values_b = projected[:, (H + KV) * HD :].reshape(row_total, KV, HD).astype(jnp.bfloat16)
    attended, log_total = attention_forward(queries, keys_b, values_b, allowed)
    middle = flat_rows + jnp.dot(attended, full_out, preferred_element_type=jnp.float32)
    normed_two, inv_two = norm_forward(middle, gain_m)
    group_rows = lax.all_gather(normed_two, "shard", axis=0, tiled=True)
    gate_pre = jnp.dot(group_rows, w_gate, preferred_element_type=jnp.float32)
    up_pre = jnp.dot(group_rows, w_up, preferred_element_type=jnp.float32)
    silu_val, silu_slope = silu_parts(gate_pre)
    activated = (silu_val * up_pre).astype(jnp.bfloat16)
    branch_out = lax.psum_scatter(
        jnp.dot(activated, w_down, preferred_element_type=jnp.float32).astype(jnp.bfloat16),
        "shard",
        scatter_dimension=0,
        tiled=True,
    ).astype(jnp.float32)
    hidden_out = (middle + branch_out).astype(jnp.bfloat16).reshape(hidden_in.shape)
    cot_rows = cotangent.reshape(row_total, D)
    cot_float = cot_rows.astype(jnp.float32)
    group_cot = lax.all_gather(cot_rows, "shard", axis=0, tiled=True)
    grad_act = jnp.dot(group_cot, w_down.T, preferred_element_type=jnp.float32)
    grad_up_b = (grad_act * silu_val).astype(jnp.bfloat16)
    grad_gate_b = (grad_act * up_pre * silu_slope).astype(jnp.bfloat16)
    own_down = jnp.dot(activated.T, group_cot, preferred_element_type=jnp.float32)
    own_gate = jnp.dot(group_rows.T, grad_gate_b, preferred_element_type=jnp.float32)
    own_up = jnp.dot(group_rows.T, grad_up_b, preferred_element_type=jnp.float32)
    grad_normed = lax.psum_scatter(
        (
            jnp.dot(grad_gate_b, w_gate.T, preferred_element_type=jnp.float32)
            + jnp.dot(grad_up_b, w_up.T, preferred_element_type=jnp.float32)
        ).astype(jnp.bfloat16),
        "shard",
        scatter_dimension=0,
        tiled=True,
    ).astype(jnp.float32)
    back_two, gain_two_grad = norm_backward(middle, inv_two, gain_m, grad_normed)
    grad_middle = cot_float + back_two
    grad_middle_b = grad_middle.astype(jnp.bfloat16)
    again_qkv, again_out = (
        lax.all_gather(w_qkv, "shard", axis=1, tiled=True),
        lax.all_gather(w_out, "shard", axis=1, tiled=True),
    )
    grad_attended = jnp.dot(grad_middle_b, again_out.T, preferred_element_type=jnp.float32).astype(
        jnp.bfloat16
    )
    grad_queries, grad_keys, grad_values = attention_backward(
        queries, keys_b, values_b, allowed, log_total, attended, grad_attended
    )
    grad_queries = rotate_back(grad_queries, cosine, sine_part)
    grad_keys = rotate_back(grad_keys, cosine, sine_part)
    grad_proj = jnp.concatenate(
        [
            grad_queries.reshape(row_total, H * HD),
            grad_keys.reshape(row_total, KV * HD),
            grad_values.reshape(row_total, KV * HD),
        ],
        1,
    ).astype(jnp.bfloat16)
    grad_normed_one = jnp.dot(grad_proj, again_qkv.T, preferred_element_type=jnp.float32)
    back_one, gain_one_grad = norm_backward(flat_rows, inv_one, gain_a, grad_normed_one)
    grad_input = (grad_middle + back_one).reshape(hidden_in.shape)
    own_qkv, own_out, own_gain_a, own_gain_m = (
        lax.psum_scatter(
            jnp.dot(normed_one.T, grad_proj, preferred_element_type=jnp.float32).astype(
                jnp.bfloat16
            ),
            "shard",
            scatter_dimension=1,
            tiled=True,
        ).astype(jnp.float32),
        lax.psum_scatter(
            jnp.dot(attended.T, grad_middle_b, preferred_element_type=jnp.float32).astype(
                jnp.bfloat16
            ),
            "shard",
            scatter_dimension=1,
            tiled=True,
        ).astype(jnp.float32),
        lax.psum_scatter(
            gain_one_grad.astype(jnp.bfloat16), "shard", scatter_dimension=0, tiled=True
        ).astype(jnp.float32),
        lax.psum_scatter(
            gain_two_grad.astype(jnp.bfloat16), "shard", scatter_dimension=0, tiled=True
        ).astype(jnp.float32),
    )
    summed = (
        lax.psum(own_qkv.astype(jnp.bfloat16), "replica").astype(jnp.float32),
        lax.psum(own_out.astype(jnp.bfloat16), "replica").astype(jnp.float32),
        lax.psum(own_gate.astype(jnp.bfloat16), "replica").astype(jnp.float32),
        lax.psum(own_up.astype(jnp.bfloat16), "replica").astype(jnp.float32),
        lax.psum(own_down.astype(jnp.bfloat16), "replica").astype(jnp.float32),
        lax.psum(own_gain_a.astype(jnp.bfloat16), "replica").astype(jnp.float32),
        lax.psum(own_gain_m.astype(jnp.bfloat16), "replica").astype(jnp.float32),
    )
    return (
        hidden_out,
        grad_input,
        summed[0],
        summed[1],
        summed[2],
        summed[3],
        summed[4],
        summed[5],
        summed[6],
    )


def solution(mesh):
    in_specs = (
        P(("shard", "replica"), None, None),
        P(("shard", "replica"), None, None),
        P(("shard", "replica"), None),
        P(("shard", "replica"), None),
        P(None, "shard"),
        P(None, "shard"),
        P(None, "shard"),
        P(None, "shard"),
        P("shard", None),
        P("shard"),
        P("shard"),
    )
    out_specs = (
        P(("shard", "replica"), None, None),
        P(("shard", "replica"), None, None),
        P(None, "shard"),
        P(None, "shard"),
        P(None, "shard"),
        P(None, "shard"),
        P("shard", None),
        P("shard"),
        P("shard"),
    )
    return jax.shard_map(
        on_device, mesh=mesh, in_specs=in_specs, out_specs=out_specs, check_vma=False
    )
```

profile of v0, /device:TPU:0, one launch (start us, length us, event | category | flops | bytes accessed | tf_op | source)
XLA Modules:
  0.0 492.3 jit_solution(3452470993920954828)
XLA Ops:
  8.0 2.1 copy.61
  13.8 11.5 %all-reduce.11 = (bf16[960]{0:T(1024)(128)(2,1)S(1)}, bf16[960]{0:T(1024)(128)(2,1)S(1)}) all-reduce(bf16[960]{0:T(1024)(128)(2,1)S(1)} %dynamic-update-slice, bf16[960]{0:T(1024)(128)(2,1)S(1)} %dynamic-update-slice.1), channel_id=1, replica_groups=mesh['shard'=4,'replica'=8] {'shard'}, use_global_device_ids=true, to_apply=%add | all-reduce | flops 1920 | bytes 7680
  27.5 30.0 %all-gather.7.cloned.1.call-done = bf16[960,1600]{0,1:T(8,128)(2,1)} async-done(((bf16[960,400]{0,1:T(8,128)(2,1)}), bf16[960,1600]{0,1:T(8,128)(2,1)}) %all-gather.7.cloned.1.call-update) | async-done | bytes 3072016 | tf_op jit(solution)/shard_map/all_gather | solution.py:133
  57.5 3.2 fusion.58
  69.4 24.7 %all-gather.9.cloned.1.call-done = bf16[960,960]{0,1:T(8,128)(2,1)} async-done(((bf16[960,240]{0,1:T(8,128)(2,1)}), bf16[960,960]{0,1:T(8,128)(2,1)}) %all-gather.9.cloned.1.call-update) | async-done | bytes 1843216 | tf_op jit(solution)/shard_map/all_gather | solution.py:134
  94.1 2.4 multiply_reduce_fusion.1
  97.7 45.5 %all-gather.11.cloned.1.call-done = bf16[1,848,960]{2,0,1:T(2,128)(2,1)} async-done(((bf16[1,212,960]{2,0,1:T(2,128)(2,1)}), bf16[1,848,960]{2,0,1:T(2,128)(2,1)}) %all-gather.11.cloned.1.call-update) | async-done | bytes 1628176 | tf_op jit(solution)/shard_map/all_gather | solution.py:164
  143.2 9.4 %copy.63 = bf16[1,848,960]{1,2,0:T(8,128)(2,1)} copy(bf16[1,848,960]{2,0,1:T(2,128)(2,1)} %all-gather.11.cloned.1.call-done) | data formatting | bytes 3256320 | tf_op jit(solution)/shard_map/all_gather | solution.py:164
  152.6 25.4 %all-gather.13.cloned.1.call-done = bf16[4,212,960]{2,1,0:T(8,128)(2,1)} async-done(((bf16[1,212,960]{2,1,0:T(8,128)(2,1)}), bf16[4,212,960]{2,1,0:T(8,128)(2,1)}) %all-gather.13.cloned.1.call-update) | async-done | bytes 1628176 | tf_op jit(solution)/shard_map/all_gather | solution.py:150
  177.9 2.8 reshape.177
  180.7 3.5 fusion.70
  185.8 2.4 multiply_convert_fusion
  188.2 2.7 convolution_convert_fusion.2
  192.5 2.7 add_convert_fusion
  195.3 65.1 %fusion.64 = (bf16[224,960]{1,0:T(8,128)(2,1)S(1)}, bf16[224,960]{1,0:T(8,128)(2,1)S(1)}) fusion(bf16[848,960]{1,0:T(8,128)(2,1)} %convolution_convert_fusion.2, bf16[848,960]{1,0:T(8,128)(2,1)} %add_convert_fusion), kind=kCustom, calls=%all-reduce-scatter.2 | all-reduce-scatter fusion | flops 1720321 | bytes 4116992
  260.4 2.4 collective-permute-start.1
  263.5 4.3 collective-permute-start
  270.7 2.6 fusion.33
  275.1 2.4 copy.77
  277.8 3.4 convolution_convert_fusion.5
  284.6 2.2 fusion.4
  291.0 2.9 convolution_convert_fusion
  295.4 4.0 fusion.16
  299.4 2.7 convolution_convert_fusion.3
  302.1 2.7 convolution_convert_fusion.4
  304.9 7.9 %reduce-scatter.11.cloned.1.call-done = bf16[240,960]{1,0:T(8,128)(2,1)} async-done(((bf16[960,960]{1,0:T(8,128)(2,1)}), bf16[240,960]{1,0:T(8,128)(2,1)}) %reduce-scatter.11.cloned.1.call-update) | async-done | bytes 460816
  314.8 45.9 %reduce-scatter.9.cloned.1.call-done = bf16[960,400]{0,1:T(8,128)(2,1)} async-done(((bf16[960,1600]{0,1:T(8,128)(2,1)}), bf16[960,400]{0,1:T(8,128)(2,1)}) %reduce-scatter.9.cloned.1.call-update) | async-done | bytes 768016 | tf_op jit(solution)/shard_map/reduce_scatter | solution.py:207
  361.9 3.1 fusion.46
  365.0 8.9 %all-reduce.10 = (bf16[960]{0:T(1024)(128)(2,1)S(1)}, bf16[960]{0:T(1024)(128)(2,1)S(1)}) all-reduce(bf16[960]{0:T(1024)(128)(2,1)S(1)} %get-tuple-element.47, bf16[960]{0:T(1024)(128)(2,1)S(1)} %get-tuple-element.45), channel_id=7, replica_groups=mesh['shard'=4,'replica'=8] {'shard'}, use_global_device_ids=true, to_apply=%region_17.18.clone | all-reduce | flops 1920 | bytes 7680
  374.1 15.1 %all-reduce.8 = (bf16[240]{0:T(256)(128)(2,1)S(1)}, bf16[240]{0:T(256)(128)(2,1)S(1)}) all-reduce(bf16[240]{0:T(256)(128)(2,1)S(1)} %dynamic-slice.7, bf16[240]{0:T(256)(128)(2,1)S(1)} %dynamic-slice.9), channel_id=1, replica_groups=mesh['shard'=4,'replica'=8] {'replica'}, use_global_device_ids=true, to_apply=%region_18.19 | all-reduce | flops 480 | bytes 1920 | tf_op jit(solution)/shard_map/psum | solution.py:236
  393.6 83.1 %all-reduce.15.cloned.1.call-done = (bf16[960,400]{0,1:T(8,128)(2,1)}, bf16[960,240]{1,0:T(8,128)(2,1)}, bf16[960,640]{1,0:T(8,128)(2,1)}, bf16[960,640]{1,0:T(8,128)(2,1)}, bf16[640,960]{0,1:T(8,128)(2,1)}) async-done(((bf16[960,400]{0,1:T(8,128)(2,1)}, bf16[960,240]{1,0:T(8,128)(2,1)}, bf16[960,640]{1,0:T(8,128)(2,1)}, bf16[960,640]{1,0:T(8,128)(2,1)}, bf16[640,960]{0,1:T(8,128)(2,1)}), ...) | async-done | bytes 4915216 | tf_op jit(solution)/shard_map/psum | solution.py:231
  476.7 2.6 convert_element_type.183
  (169 shorter events, 46.1 us)
Async XLA Ops:
  7.2 178.6 %copy-start = (bf16[640,960]{0,1:T(8,128)(2,1)S(1)}, bf16[640,960]{0,1:T(8,128)(2,1)}, u32[]{:S(2)}) copy-start(bf16[640,960]{0,1:T(8,128)(2,1)} %param.19) | copy-start | bytes 3686404
  7.2 3.0 copy-start.11
  7.2 50.3 %all-gather.7.cloned.1.call-start = ((), (), s32[]{:S(2)}) async-start(), calls=%async_computation.2 | async-start | bytes 4096000 | tf_op jit(solution)/shard_map/all_gather | solution.py:133
  7.9 3.9 copy-start.34
  7.9 3.9 copy-start.5
  8.0 86.2 %all-gather.9.cloned.1.call-start = ((), (), s32[]{:S(2)}) async-start(), calls=%async_computation.3 | async-start | bytes 2457600 | tf_op jit(solution)/shard_map/all_gather | solution.py:134
  10.1 2.0 copy-start.32
  10.1 3.3 copy-start.37
  10.1 3.5 copy-start.38
  10.1 16.7 %copy-start.33 = (s32[1,212]{1,0:T(1,128)S(1)}, s32[1,212]{1,0:T(1,128)}, u32[]{:S(2)}) copy-start(s32[1,212]{1,0:T(1,128)} %param.13) | copy-start | bytes 2548
  10.1 133.1 %all-gather.11.cloned.1.call-start = ((), (), s32[]{:S(2)}) async-start(), calls=%async_computation.5 | async-start | bytes 4341760 | tf_op jit(solution)/shard_map/all_gather | solution.py:164
  11.8 166.2 %all-gather.13.cloned.1.call-start = ((), (), s32[]{:S(2)}) async-start(), calls=%async_computation.6 | async-start | bytes 2211840 | tf_op jit(solution)/shard_map/all_gather | solution.py:150
  63.0 2.3 copy-start.16
  63.0 2.3 copy-start.17
  69.4 203.8 %copy-start.10 = (bf16[5,64,3,212]{3,1,2,0:T(8,128)(2,1)}, bf16[5,64,3,212]{3,1,2,0:T(8,128)(2,1)S(1)}, u32[]{:S(2)}) copy-start(bf16[5,64,3,212]{3,1,2,0:T(8,128)(2,1)S(1)} %fusion.19) | copy-start | bytes 1221124
  97.5 215.3 %reduce-scatter.11.cloned.1.call-start = ((), (), s32[]{:S(2)}) async-start(), calls=%async_computation.7 | async-start | bytes 2457600
  180.7 3.5 copy-start.12
  180.7 3.5 copy-start.35
  188.2 2.8 copy-start.43
  188.2 2.8 copy-start.41
  188.2 4.3 copy-start.39
  260.4 7.4 %collective-permute-start.1 = (bf16[36,960]{1,0:T(8,128)(2,1)S(1)}, bf16[36,960]{1,0:T(8,128)(2,1)S(1)}, u32[]{:S(2)}, u32[]{:S(2)}) collective-permute-start(bf16[36,960]{1,0:T(8,128)(2,1)S(1)} %slice.57), channel_id=1, source_target_pairs={{0,8},{8,16},{16,24},{1,9},{9,17},{17,25},{2,10},{10,18},{18,26},{... | collective-permute-start | bytes 207368
  263.5 6.3 %collective-permute-start = (bf16[36,960]{1,0:T(8,128)(2,1)S(1)}, bf16[36,960]{1,0:T(8,128)(2,1)S(1)}, u32[]{:S(2)}, u32[]{:S(2)}) collective-permute-start(bf16[36,960]{1,0:T(8,128)(2,1)S(1)} %slice.56), channel_id=1, source_target_pairs={{0,8},{8,16},{16,24},{1,9},{9,17},{17,25},{2,10},{10,18},{18,26},{... | collective-permute-start | bytes 207368
  277.5 83.1 %reduce-scatter.9.cloned.1.call-start = ((), (), s32[]{:S(2)}) async-start(), calls=%async_computation.4 | async-start | bytes 4096000 | tf_op jit(solution)/shard_map/reduce_scatter | solution.py:207
  277.8 6.7 %copy-start.3 = (f32[5,3,212,212]{2,3,1,0:T(8,128)S(1)}, f32[5,3,212,212]{2,3,1,0:T(8,128)}, u32[]{:S(2)}) copy-start(f32[5,3,212,212]{2,3,1,0:T(8,128)} %copy-done.2) | copy-start | bytes 8089924
  284.5 2.2 copy-start.19
  294.0 5.4 %copy-start.13 = (bf16[848,960]{1,0:T(8,128)(2,1)S(1)}, bf16[848,960]{1,0:T(8,128)(2,1)}, u32[]{:S(2)}) copy-start(bf16[848,960]{1,0:T(8,128)(2,1)} %reshape.177) | copy-start | bytes 4884484
  294.0 182.8 %all-reduce.15.cloned.1.call-start = ((), (), s32[]{:S(2)}) async-start(), calls=%async_computation.8 | async-start | bytes 9994240 | tf_op jit(solution)/shard_map/psum | solution.py:231
  295.4 4.0 copy-start.40
  299.4 2.7 copy-start.42
  476.7 2.6 copy-start.26
  476.7 3.6 copy-start.22
  (21 other events, 27.3 us)
Sparse Core Ops, SparseCore 0:
  9.9 47.6 all-gather.6
  60.0 34.1 all-gather.8
  96.5 46.5 all-gather.10
  145.4 32.4 all-gather.12
  277.6 35.0 reduce-scatter.10
  315.6 44.9 reduce-scatter.8
  364.0 112.6 all-reduce.14
where the time goes:
time: 494 us; the launch traced here: 492 us
  waiting for transfers between devices  264 us (53%)
  blocking collectives  101 us (20%)
  matrix products  46 us (9%)
  local copies, waits for them, and re-layouts  35.4 us (7%)
  other arithmetic  22.2 us (4%)
  between operations  16.8 us (3%)
  starting transfers between devices  7.37 us (1%)
    unnamed x3, blocking collectives  85.5 us
    psum x1, waiting for transfers between devices, on_device(): lax.psum(own_qkv.astype(jnp.bfloat16), 'replica').astype(jnp.float32)  83.1 us
    reduce_scatter x1, waiting for transfers between devices, on_device(): lax.psum_scatter(jnp.dot(normed_one.T, grad_proj, preferred_element_type=...  45.9 us
    all_gather x1, waiting for transfers between devices, on_device(): group_cot = lax.all_gather(cot_rows, 'shard', axis=0, tiled=True)  45.5 us
    all_gather x1, waiting for transfers between devices, on_device(): lax.all_gather(w_qkv, 'shard', axis=1, tiled=True)  30 us
    all_gather x1, waiting for transfers between devices, on_device(): group_rows = lax.all_gather(normed_two, 'shard', axis=0, tiled=True)  25.4 us
    all_gather x1, waiting for transfers between devices, on_device(): lax.all_gather(w_out, 'shard', axis=1, tiled=True)  24.7 us
    unnamed x105, local copies, waits for them, and re-layouts  21.8 us
  transfers between devices with their start and end apart: 9, of which 8 were waited for; matrix products, arithmetic and copies ran while one was open for 13% of the time, Pallas kernels for 0%

commit v1 on v0

--- a/solution.py
+++ b/solution.py
@@ -1,3 +1,4 @@
+import functools
 import math
 import jax
 import jax.numpy as jnp
@@ -12,6 +13,32 @@
 EPSILON = 1e-05
 THETA_BASE = 100000.0
 NEG_FILL = -1e30
+
+
+def notes_move(local_array, array_axis):
+    low, d_next, p_next = (
+        jax.lax.psum(1, axis_name="shard"),
+        jax.lax.axis_index("shard"),
+        local_array.shape[array_axis],
+    )
+    line_up = []
+    for t, kk in enumerate(local_array.shape):
+        line_up.append(kk * low if t == array_axis else kk)
+    known = lax.dynamic_update_slice_in_dim(
+        jnp.zeros(line_up, local_array.dtype), local_array, d_next * p_next, axis=array_axis
+    )
+    for d in range(1, low):
+        pool = []
+        for t in range(low):
+            pool.append((t, (t + 1) % low))
+        local_array = jax.lax.ppermute(local_array, axis_name="shard", perm=pool)
+        known = lax.dynamic_update_slice_in_dim(
+            known, local_array, (d_next - d) % low * p_next, axis=array_axis
+        )
+    return known
+
+
+classes_end = functools.partial(notes_move, array_axis=0)
 
 
 def rope_tables(position_ids):
@@ -161,7 +188,7 @@
     hidden_out = (middle + branch_out).astype(jnp.bfloat16).reshape(hidden_in.shape)
     cot_rows = cotangent.reshape(row_total, D)
     cot_float = cot_rows.astype(jnp.float32)
-    group_cot = lax.all_gather(cot_rows, "shard", axis=0, tiled=True)
+    group_cot = classes_end(cot_rows)
     grad_act = jnp.dot(group_cot, w_down.T, preferred_element_type=jnp.float32)
     grad_up_b = (grad_act * silu_val).astype(jnp.bfloat16)
     grad_gate_b = (grad_act * up_pre * silu_slope).astype(jnp.bfloat16)

time: 494 us -> 460 us (0.931)
  waiting for transfers between devices: 264 us -> 223 us
  starting transfers between devices: 7.37 us -> 12.6 us
    all_gather x1 -> x0, waiting for transfers between devices: 45.5 us -> none  [on_device(): group_cot = lax.all_gather(cot_rows, 'shard', axis=0, tiled=True)]
    ppermute x0 -> x3, waiting for transfers between devices: none -> 27.7 us  [notes_move(): local_array = jax.lax.ppermute(local_array, axis_name='shard', perm=pool)]
    all_gather x1, waiting for transfers between devices: 25.4 us -> 0.01 us  [on_device(): group_rows = lax.all_gather(normed_two, 'shard', axis=0, tiled=True)]
    dynamic_update_slice x0 -> x4, local copies, waits for them, and re-layouts: none -> 13.5 us  [the longest x3 10.2 us: notes_move(): lax.dynamic_update_slice_in_dim(known, local_array, (d_next - d) % low *...]
    all_gather x1 -> x0, local copies, waits for them, and re-layouts: 9.42 us -> none  [on_device(): group_cot = lax.all_gather(cot_rows, 'shard', axis=0, tiled=True)]
    ppermute x0 -> x3, starting transfers between devices: none -> 5.97 us  [notes_move(): local_array = jax.lax.ppermute(local_array, axis_name='shard', perm=pool)]
    unnamed x105 -> x106, local copies, waits for them, and re-layouts: 21.8 us -> 20.9 us
  transfers between devices with their start and end apart: 9 -> 11, of which waited for: 8 -> 9; matrix products, arithmetic and copies ran while one was open for 13% -> 14% of each run, Pallas kernels for 0% -> 0%
where the time goes in v1:
time: 460 us; the launch traced here: 459 us
  waiting for transfers between devices  223 us (48%)
  blocking collectives  98.7 us (21%)
  matrix products  45.7 us (10%)
  local copies, waits for them, and re-layouts  40 us (9%)
  other arithmetic  22.2 us (5%)
  between operations  16.8 us (4%)
  starting transfers between devices  12.6 us (3%)
    unnamed x3, blocking collectives  83.6 us
    psum x1, waiting for transfers between devices, on_device(): lax.psum(own_qkv.astype(jnp.bfloat16), 'replica').astype(jnp.float32)  83 us
    reduce_scatter x1, waiting for transfers between devices, on_device(): lax.psum_scatter(jnp.dot(normed_one.T, grad_proj, preferred_element_type=...  45.9 us
    all_gather x1, waiting for transfers between devices, on_device(): lax.all_gather(w_qkv, 'shard', axis=1, tiled=True)  31.8 us
    ppermute x3, waiting for transfers between devices, notes_move(): local_array = jax.lax.ppermute(local_array, axis_name='shard', perm=pool)  27.7 us
    all_gather x1, waiting for transfers between devices, on_device(): lax.all_gather(w_out, 'shard', axis=1, tiled=True)  24.7 us
    unnamed x106, local copies, waits for them, and re-layouts  20.9 us
    psum x1, blocking collectives, on_device(): lax.psum(own_gain_a.astype(jnp.bfloat16), 'replica').astype(jnp.float32)  15.1 us
  transfers between devices with their start and end apart: 11, of which 9 were waited for; matrix products, arithmetic and copies ran while one was open for 14% of the time, Pallas kernels for 0%

profile of v1, /device:TPU:0, one launch (start us, length us, event | category | flops | bytes accessed | tf_op | source)
XLA Modules:
  0.0 458.5 jit_solution(6219891576613478770)
XLA Ops:
  12.1 11.5 %all-reduce.11 = (bf16[960]{0:T(1024)(128)(2,1)S(1)}, bf16[960]{0:T(1024)(128)(2,1)S(1)}) all-reduce(bf16[960]{0:T(1024)(128)(2,1)S(1)} %dynamic-update-slice, bf16[960]{0:T(1024)(128)(2,1)S(1)} %dynamic-update-slice.1), channel_id=1, replica_groups=mesh['shard'=4,'replica'=8] {'shard'}, use_global_device_ids=true, to_apply=%add | all-reduce | flops 1920 | bytes 7680
  25.8 31.8 %all-gather.5.cloned.1.call-done = bf16[960,1600]{0,1:T(8,128)(2,1)} async-done(((bf16[960,400]{0,1:T(8,128)(2,1)}), bf16[960,1600]{0,1:T(8,128)(2,1)}) %all-gather.5.cloned.1.call-update) | async-done | bytes 3072016 | tf_op jit(solution)/shard_map/all_gather | solution.py:160
  57.6 3.2 fusion.51
  69.4 24.7 %all-gather.7.cloned.1.call-done = bf16[960,960]{0,1:T(8,128)(2,1)} async-done(((bf16[960,240]{0,1:T(8,128)(2,1)}), bf16[960,960]{0,1:T(8,128)(2,1)}) %all-gather.7.cloned.1.call-update) | async-done | bytes 1843216 | tf_op jit(solution)/shard_map/all_gather | solution.py:161
  94.2 2.4 multiply_reduce_fusion.1
  99.1 14.0 %collective-permute-done = bf16[212,960]{1,0:T(8,128)(2,1)S(1)} collective-permute-done((bf16[212,960]{1,0:T(8,128)(2,1)S(1)}, bf16[212,960]{1,0:T(8,128)(2,1)S(1)}, u32[]{:S(2)}, u32[]{:S(2)}) %collective-permute-start) | collective-permute-done | bytes 407072 | tf_op jit(solution)/shard_map/ppermute | solution.py:34
  115.7 12.1 %collective-permute-done.1 = bf16[212,960]{1,0:T(8,128)(2,1)} collective-permute-done((bf16[212,960]{1,0:T(8,128)(2,1)S(1)}, bf16[212,960]{1,0:T(8,128)(2,1)}, u32[]{:S(2)}, u32[]{:S(2)}) %collective-permute-start.1) | collective-permute-done | bytes 407072 | tf_op jit(solution)/shard_map/ppermute | solution.py:34
  127.7 2.6 collective-permute-start.2
  131.7 3.3 dynamic_update_slice.12
  135.1 3.3 dynamic_update_slice.13
  138.4 3.4 dynamic_update_slice.14
  143.5 3.4 dynamic_update_slice.15
  147.0 2.8 reshape.175
  149.8 3.5 fusion.63
  157.0 2.7 convolution_convert_fusion.2
  161.3 2.8 add_convert_fusion
  164.0 63.2 %fusion.57 = (bf16[224,960]{1,0:T(8,128)(2,1)S(1)}, bf16[224,960]{1,0:T(8,128)(2,1)S(1)}) fusion(bf16[848,960]{1,0:T(8,128)(2,1)} %convolution_convert_fusion.2, bf16[848,960]{1,0:T(8,128)(2,1)} %add_convert_fusion), kind=kCustom, calls=%all-reduce-scatter.2 | all-reduce-scatter fusion | flops 1720321 | bytes 4116992
  229.3 4.9 %collective-permute-start.3 = (bf16[36,960]{1,0:T(8,128)(2,1)S(1)}, bf16[36,960]{1,0:T(8,128)(2,1)S(1)}, u32[]{:S(2)}, u32[]{:S(2)}) collective-permute-start(bf16[36,960]{1,0:T(8,128)(2,1)S(1)} %slice.56), channel_id=1, source_target_pairs={{0,8},{8,16},{16,24},{1,9},{9,17},{17,25},{2,10},{10,18},{18,26},{... | collective-permute-start | bytes 207368
  237.1 2.6 fusion.26
  241.5 2.4 copy.63
  244.2 3.4 convolution_convert_fusion.6
  257.4 2.8 convolution_convert_fusion
  261.7 4.0 convolution_convert_fusion.3
  265.7 2.7 convolution_convert_fusion.4
  268.5 2.7 convolution_convert_fusion.5
  271.2 7.9 %reduce-scatter.11.cloned.1.call-done = bf16[240,960]{1,0:T(8,128)(2,1)} async-done(((bf16[960,960]{1,0:T(8,128)(2,1)}), bf16[240,960]{1,0:T(8,128)(2,1)}) %reduce-scatter.11.cloned.1.call-update) | async-done | bytes 460816
  281.1 45.9 %reduce-scatter.9.cloned.1.call-done = bf16[960,400]{0,1:T(8,128)(2,1)} async-done(((bf16[960,1600]{0,1:T(8,128)(2,1)}), bf16[960,400]{0,1:T(8,128)(2,1)}) %reduce-scatter.9.cloned.1.call-update) | async-done | bytes 768016 | tf_op jit(solution)/shard_map/reduce_scatter | solution.py:234
  328.2 3.1 fusion.39
  331.3 8.9 %all-reduce.10 = (bf16[960]{0:T(1024)(128)(2,1)S(1)}, bf16[960]{0:T(1024)(128)(2,1)S(1)}) all-reduce(bf16[960]{0:T(1024)(128)(2,1)S(1)} %get-tuple-element.38, bf16[960]{0:T(1024)(128)(2,1)S(1)} %get-tuple-element.36), channel_id=6, replica_groups=mesh['shard'=4,'replica'=8] {'shard'}, use_global_device_ids=true, to_apply=%region_17.18.clone | all-reduce | flops 1920 | bytes 7680
  340.4 15.1 %all-reduce.8 = (bf16[240]{0:T(256)(128)(2,1)S(1)}, bf16[240]{0:T(256)(128)(2,1)S(1)}) all-reduce(bf16[240]{0:T(256)(128)(2,1)S(1)} %dynamic-slice.7, bf16[240]{0:T(256)(128)(2,1)S(1)} %dynamic-slice.9), channel_id=1, replica_groups=mesh['shard'=4,'replica'=8] {'replica'}, use_global_device_ids=true, to_apply=%region_18.19 | all-reduce | flops 480 | bytes 1920 | tf_op jit(solution)/shard_map/psum | solution.py:263
  359.9 83.0 %all-reduce.15.cloned.1.call-done = (bf16[960,400]{0,1:T(8,128)(2,1)}, bf16[960,240]{1,0:T(8,128)(2,1)}, bf16[960,640]{1,0:T(8,128)(2,1)}, bf16[960,640]{1,0:T(8,128)(2,1)}, bf16[640,960]{0,1:T(8,128)(2,1)}) async-done(((bf16[960,400]{0,1:T(8,128)(2,1)}, bf16[960,240]{1,0:T(8,128)(2,1)}, bf16[960,640]{1,0:T(8,128)(2,1)}, bf16[960,640]{1,0:T(8,128)(2,1)}, bf16[640,960]{0,1:T(8,128)(2,1)}), ...) | async-done | bytes 4915216 | tf_op jit(solution)/shard_map/psum | solution.py:258
  442.9 2.6 convert_element_type.183
  (177 shorter events, 59.0 us)
Async XLA Ops:
  7.2 147.6 %copy-start = (bf16[640,960]{0,1:T(8,128)(2,1)S(1)}, bf16[640,960]{0,1:T(8,128)(2,1)}, u32[]{:S(2)}) copy-start(bf16[640,960]{0,1:T(8,128)(2,1)} %param.19) | copy-start | bytes 3686404
  7.2 3.2 copy-start.33
  7.2 3.0 copy-start.35
  7.2 3.0 copy-start.5
  7.2 4.4 copy-start.38
  7.2 4.7 %copy-start.39 = (bf16[240]{0:T(256)(128)(2,1)S(1)}, bf16[240]{0:T(256)(128)(2,1)}, u32[]{:S(2)}) copy-start(bf16[240]{0:T(256)(128)(2,1)} %param.21) | copy-start | bytes 1444
  7.2 17.8 %copy-start.34 = (s32[1,212]{1,0:T(1,128)S(1)}, s32[1,212]{1,0:T(1,128)}, u32[]{:S(2)}) copy-start(s32[1,212]{1,0:T(1,128)} %param.13) | copy-start | bytes 2548
  7.3 50.3 %all-gather.5.cloned.1.call-start = ((), (), s32[]{:S(2)}) async-start(), calls=%async_computation.2 | async-start | bytes 4096000 | tf_op jit(solution)/shard_map/all_gather | solution.py:160
  8.0 86.2 %all-gather.7.cloned.1.call-start = ((), (), s32[]{:S(2)}) async-start(), calls=%async_computation.3 | async-start | bytes 2457600 | tf_op jit(solution)/shard_map/all_gather | solution.py:161
  10.1 136.9 %all-gather.9.cloned.1.call-start = ((), (), s32[]{:S(2)}) async-start(), calls=%async_computation.5 | async-start | bytes 2211840 | tf_op jit(solution)/shard_map/all_gather | solution.py:177
  63.1 2.3 copy-start.16
  63.1 2.3 copy-start.17
  69.4 170.2 %copy-start.10 = (bf16[5,64,3,212]{3,1,2,0:T(8,128)(2,1)}, bf16[5,64,3,212]{3,1,2,0:T(8,128)(2,1)S(1)}, u32[]{:S(2)}) copy-start(bf16[5,64,3,212]{3,1,2,0:T(8,128)(2,1)S(1)} %fusion.12) | copy-start | bytes 1221124
  97.5 181.6 %reduce-scatter.11.cloned.1.call-start = ((), (), s32[]{:S(2)}) async-start(), calls=%async_computation.6 | async-start | bytes 2457600
  97.6 15.5 %collective-permute-start = (bf16[212,960]{1,0:T(8,128)(2,1)S(1)}, bf16[212,960]{1,0:T(8,128)(2,1)S(1)}, u32[]{:S(2)}, u32[]{:S(2)}) collective-permute-start(bf16[212,960]{1,0:T(8,128)(2,1)S(1)} %bitcast.134), channel_id=1, source_target_pairs={{0,8},{8,16},{16,24},{24,0},{1,9},{9,17},{17,25},{25,1},{2,10},{10... | collective-permute-start | bytes 1221128 | tf_op jit(solution)/shard_map/ppermute | solution.py:34
  113.8 13.9 %collective-permute-start.1 = (bf16[212,960]{1,0:T(8,128)(2,1)S(1)}, bf16[212,960]{1,0:T(8,128)(2,1)}, u32[]{:S(2)}, u32[]{:S(2)}) collective-permute-start(bf16[212,960]{1,0:T(8,128)(2,1)S(1)} %collective-permute-done), channel_id=1, source_target_pairs={{0,8},{8,16},{16,24},{24,0},{1,9},{9,17},{17,25},{25,1},{2,10},{10... | collective-permute-start | bytes 1221128 | tf_op jit(solution)/shard_map/ppermute | solution.py:34
  127.7 15.8 %collective-permute-start.2 = (bf16[212,960]{1,0:T(8,128)(2,1)}, bf16[212,960]{1,0:T(8,128)(2,1)}, u32[]{:S(2)}, u32[]{:S(2)}) collective-permute-start(bf16[212,960]{1,0:T(8,128)(2,1)} %collective-permute-done.1), channel_id=1, source_target_pairs={{0,8},{8,16},{16,24},{24,0},{1,9},{9,17},{17,25},{25,1},{2,10},{10... | collective-permute-start | bytes 1221128 | tf_op jit(solution)/shard_map/ppermute | solution.py:34
  149.8 3.5 copy-start.14
  149.8 3.5 copy-start.36
  156.9 2.8 copy-start.44
  156.9 2.8 copy-start.42
  156.9 4.3 copy-start.40
  227.3 6.9 %collective-permute-start.4 = (bf16[36,960]{1,0:T(8,128)(2,1)S(1)}, bf16[36,960]{1,0:T(8,128)(2,1)S(1)}, u32[]{:S(2)}, u32[]{:S(2)}) collective-permute-start(bf16[36,960]{1,0:T(8,128)(2,1)S(1)} %slice.57), channel_id=1, source_target_pairs={{0,8},{8,16},{16,24},{1,9},{9,17},{17,25},{2,10},{10,18},{18,26},{... | collective-permute-start | bytes 207368
  229.3 6.9 %collective-permute-start.3 = (bf16[36,960]{1,0:T(8,128)(2,1)S(1)}, bf16[36,960]{1,0:T(8,128)(2,1)S(1)}, u32[]{:S(2)}, u32[]{:S(2)}) collective-permute-start(bf16[36,960]{1,0:T(8,128)(2,1)S(1)} %slice.56), channel_id=1, source_target_pairs={{0,8},{8,16},{16,24},{1,9},{9,17},{17,25},{2,10},{10,18},{18,26},{... | collective-permute-start | bytes 207368
  243.9 83.1 %reduce-scatter.9.cloned.1.call-start = ((), (), s32[]{:S(2)}) async-start(), calls=%async_computation.4 | async-start | bytes 4096000 | tf_op jit(solution)/shard_map/reduce_scatter | solution.py:234
  244.2 6.7 %copy-start.3 = (f32[5,3,212,212]{2,3,1,0:T(8,128)S(1)}, f32[5,3,212,212]{2,3,1,0:T(8,128)}, u32[]{:S(2)}) copy-start(f32[5,3,212,212]{2,3,1,0:T(8,128)} %copy-done.2) | copy-start | bytes 8089924
  260.2 5.5 %copy-start.15 = (bf16[848,960]{1,0:T(8,128)(2,1)S(1)}, bf16[848,960]{1,0:T(8,128)(2,1)}, u32[]{:S(2)}) copy-start(bf16[848,960]{1,0:T(8,128)(2,1)} %reshape.175) | copy-start | bytes 4884484
  260.2 182.7 %all-reduce.15.cloned.1.call-start = ((), (), s32[]{:S(2)}) async-start(), calls=%async_computation.7 | async-start | bytes 9994240 | tf_op jit(solution)/shard_map/psum | solution.py:258
  261.7 4.0 copy-start.41
  265.7 2.7 copy-start.43
  442.9 2.6 copy-start.26
  442.9 3.6 copy-start.22
  (24 other events, 31.0 us)
Sparse Core Ops, SparseCore 0:
  9.9 47.6 all-gather.4
  60.0 34.0 all-gather.6
  97.6 42.9 all-gather.8
  244.0 35.0 reduce-scatter.10
  282.0 44.9 reduce-scatter.8
  330.2 112.6 all-reduce.14
